TPU v7x, 512 devices: a whole 4x8x8 slice. The times are simulated.
512 devices in a mesh: wide: 64 (over y, z), narrow: 8 (over x, core).
Axes of the slice: x: 4, y: 8, z: 8, core: 2. Of those that a mesh axis runs over, the one named last changes fastest.
Arguments:
- hidden: bfloat16 [16384, 1536], P('wide', 'narrow'), may hold values from -6 to 6
- start_state: bfloat16 [1024, 24, 64, 128], P('wide', 'narrow'), may hold values from -0.59765625 to 0.59765625
- tail_inner: bfloat16 [1024, 3, 1536], P('wide', None, 'narrow'), may hold values from -6 to 6
- tail_shared: bfloat16 [1024, 3, 256], P('wide'), may hold values from -6 to 6
- input_gain: float32 [1536], replicated, may hold values from 0.5 to 1.5
- w_gate_inner: bfloat16 [1536, 3072], P(None, 'narrow'), may hold values from -0.15625 to 0.15625
- w_shared: bfloat16 [1536, 256], P(None, 'narrow'), may hold values from -0.15625 to 0.15625
- w_step: bfloat16 [1536, 24], P(None, 'narrow'), may hold values from -0.15625 to 0.15625
- step_bias: float32 [24], P('narrow'), may hold values from -4 to -1
- decay_log: float32 [24], P('narrow'), may hold values from 0 to 2.5
- conv_inner: bfloat16 [4, 1536], P(None, 'narrow'), may hold values from -3 to 3
- conv_inner_bias: float32 [1536], P('narrow'), may hold values from -1.5 to 1.5
- conv_shared: bfloat16 [4, 256], replicated, may hold values from -3 to 3
- conv_shared_bias: float32 [256], replicated, may hold values from -1.5 to 1.5
- skip_gain: float32 [24], P('narrow'), may hold values from 0.5 to 1.5
- gated_gain: float32 [1536], P('narrow'), may hold values from 0.5 to 1.5
- w_output: bfloat16 [1536, 1536], P('narrow'), may hold values from -0.15625 to 0.15625
- next_gain: float32 [1536], replicated, may hold values from 0.5 to 1.5
- w_next: bfloat16 [1536, 3224], P(None, 'narrow'), may hold values from -0.15625 to 0.15625
- dealing: int32 [1024], replicated, may hold values from 0 to 1023, as said below
- accepted: int32 [1024], replicated, may hold values from 0 to 16
- owners: int32 [1024], replicated, may hold values from 0 to 63, as said below
Outputs:
- new_hidden: bfloat16 [16384, 1536], P('wide', 'narrow')
- next_input: bfloat16 [16384, 3224], P('wide', 'narrow')
- kept_state: bfloat16 [1024, 24, 64, 128], P('wide', 'narrow')
- kept_tail_inner: bfloat16 [1024, 3, 1536], P('wide', None, 'narrow')
- kept_tail_shared: bfloat16 [1024, 3, 256], P('wide')
Inputs may be any that keep to these rules, and one draw needn't show every extreme that they name: `dealing`: a permutation of the 1024 requests; slot j lies on index j // 16 of wide. Each owner keeps exactly 16 requests, and the requests of the slots of one index of wide have different owners.
All inputs are finite; a program needn't handle non-finite values.
Results may differ from a plain program's by a relative error of at most 0.02.
Values may be sent and summed in bfloat16 or wider, within the bound.
A program may use at most 64 MiB of HBM per device.

v0:
```python
import jax
import jax.numpy as jnp
from jax import lax
from jax.sharding import PartitionSpec as P

EPSILON = 1e-05
HIGHEST = lax.Precision.HIGHEST


def root_norm(values, gain):
    values = values.astype(jnp.float32)
    factor = lax.rsqrt(jnp.mean(values * values, axis=-1, keepdims=True) + EPSILON)
    return (values * factor * gain).astype(jnp.bfloat16)


def causal_filter(tail, fresh, weight, offset):
    extended = jnp.concatenate([tail, fresh], axis=1)
    length = fresh.shape[1]
    summed = jnp.zeros(fresh.shape, jnp.float32) + offset
    for place in range(weight.shape[0]):
        summed = summed + extended[:, place : place + length].astype(jnp.float32) * weight[
            place
        ].astype(jnp.float32)
    return (jax.nn.silu(summed), extended)


def pick_rows(extended, accepted_now, count):
    length = extended.shape[1]
    wanted = accepted_now[:, None] + jnp.arange(count, dtype=jnp.int32)[None, :]
    onehot = (wanted[:, :, None] == jnp.arange(length, dtype=jnp.int32)[None, None, :]).astype(
        jnp.float32
    )
    return jnp.einsum(
        "rqe,rec->rqc", onehot, extended.astype(jnp.float32), precision=HIGHEST
    ).astype(jnp.bfloat16)


def state_block(
    inner, shared, step_raw, step_bias, decay_log, skip_gain, start_state, accepted_now
):
    states = shared.shape[-1] // 2
    b_part = shared[..., :states]
    c_part = shared[..., states:]
    length = inner.shape[1]
    steps_now = jax.nn.softplus(step_raw.astype(jnp.float32) + step_bias)
    log_decay = steps_now * -jnp.exp(decay_log)
    cumul = jnp.cumsum(log_decay, axis=1)
    prefix = jnp.concatenate([jnp.zeros_like(cumul[:, :1]), cumul], axis=1)
    places = jnp.arange(length, dtype=jnp.int32)
    lower = (places[:, None] >= places[None, :])[None, :, :, None]
    spread = cumul[:, :, None, :] - cumul[:, None, :, :]
    weights = (
        jnp.where(lower, jnp.exp(jnp.where(lower, spread, 0.0)), 0.0) * steps_now[:, None, :, :]
    )
    intersection = jnp.einsum("rtn,rsn->rts", c_part, b_part, precision=HIGHEST)
    mixing = weights * intersection[:, :, :, None]
    state_now = start_state.astype(jnp.float32)
    carried = (
        jnp.einsum("rtn,rhpn->rthp", c_part, state_now, precision=HIGHEST)
        * jnp.exp(cumul)[:, :, :, None]
    )
    direct = jnp.einsum("rtsh,rshp->rthp", mixing, inner, precision=HIGHEST)
    outputs = carried + direct + skip_gain[:, None] * inner
    chosen = (jnp.arange(length + 1, dtype=jnp.int32)[None, :] == accepted_now[:, None]).astype(
        jnp.float32
    )
    ending = jnp.einsum("rk,rkh->rh", chosen, prefix, precision=HIGHEST)
    before = (places[None, :] < accepted_now[:, None])[:, :, None]
    factor = (
        jnp.where(before, jnp.exp(jnp.where(before, ending[:, None, :] - cumul, 0.0)), 0.0)
        * steps_now
    )
    kept = jnp.exp(ending)[:, :, None, None] * state_now + jnp.einsum(
        "rsh,rshp,rsn->rhpn", factor, inner, b_part, precision=HIGHEST
    )
    return (outputs, kept.astype(jnp.bfloat16))


def local(
    hidden,
    start_state,
    tail_inner,
    tail_shared,
    input_gain,
    w_gate_inner,
    w_shared,
    w_step,
    step_bias,
    decay_log,
    conv_inner,
    conv_inner_bias,
    conv_shared,
    conv_shared_bias,
    skip_gain,
    gated_gain,
    w_output,
    next_gain,
    w_next,
    dealing,
    accepted,
    owners,
):
    wide_index = lax.axis_index("wide")
    wide_count = lax.axis_size("wide")
    narrow_count = lax.axis_size("narrow")
    full_rows = lax.all_gather(hidden, "narrow", axis=1, tiled=True)
    normed_in = root_norm(full_rows, input_gain)
    tokens = full_rows.shape[0]
    requests = start_state.shape[0]
    length = tokens // requests
    heads_here = w_step.shape[1]
    head_size = start_state.shape[2]
    block = w_output.shape[0]
    gate_inner = jnp.dot(normed_in, w_gate_inner, preferred_element_type=jnp.float32).astype(
        jnp.bfloat16
    )
    shared_piece = jnp.dot(normed_in, w_shared, preferred_element_type=jnp.float32).astype(
        jnp.bfloat16
    )
    step_raw = jnp.dot(normed_in, w_step, preferred_element_type=jnp.float32).astype(jnp.bfloat16)
    shared_in = lax.all_gather(shared_piece, "narrow", axis=1, tiled=True)
    gate_part = gate_inner[:, :block]
    inner_in = gate_inner[:, block:]
    inner_conv, inner_ext = causal_filter(
        tail_inner, inner_in.reshape(requests, length, block), conv_inner, conv_inner_bias
    )
    shared_conv, shared_ext = causal_filter(
        tail_shared, shared_in.reshape(requests, length, -1), conv_shared, conv_shared_bias
    )
    first_slot = wide_index * requests
    slot_requests = lax.dynamic_slice_in_dim(dealing, first_slot, requests)
    accepted_now = jnp.take(accepted, slot_requests)
    outputs, kept = state_block(
        inner_conv.reshape(requests, length, heads_here, head_size),
        shared_conv,
        step_raw.reshape(requests, length, heads_here),
        step_bias,
        decay_log,
        skip_gain,
        start_state,
        accepted_now,
    )
    gated = outputs.reshape(tokens, block) * jax.nn.silu(gate_part.astype(jnp.float32))
    squares = lax.psum(jnp.sum(gated * gated, axis=1, keepdims=True), "narrow")
    gated_norm = (
        gated * lax.rsqrt(squares / (block * narrow_count) + EPSILON) * gated_gain
    ).astype(jnp.bfloat16)
    partial_sum = jnp.dot(gated_norm, w_output, preferred_element_type=jnp.float32)
    whole_sum = lax.psum(partial_sum.astype(jnp.bfloat16), "narrow").astype(jnp.float32)
    new_full = (full_rows.astype(jnp.float32) + whole_sum).astype(jnp.bfloat16)
    new_part = lax.dynamic_slice_in_dim(
        new_full, lax.axis_index("narrow") * hidden.shape[1], hidden.shape[1], 1
    )
    normed_next = root_norm(new_full, next_gain)
    next_input = jnp.dot(normed_next, w_next, preferred_element_type=jnp.float32).astype(
        jnp.bfloat16
    )
    owner_table = (owners[:, None] == jnp.arange(wide_count, dtype=jnp.int32)[None, :]).astype(
        jnp.int32
    )
    ranking = jnp.sum((jnp.cumsum(owner_table, axis=0) - owner_table) * owner_table, axis=1)
    slot_owner = jnp.take(owners, dealing)
    slot_rank = jnp.take(ranking, dealing)
    local_owner = lax.dynamic_slice_in_dim(slot_owner, first_slot, requests)
    send_table = (jnp.arange(wide_count, dtype=jnp.int32)[:, None] == local_owner[None, :]).astype(
        jnp.bfloat16
    )
    state_bucket = (
        jnp.dot(send_table, kept.reshape(requests, -1), preferred_element_type=jnp.float32)
        .astype(jnp.bfloat16)
        .reshape((wide_count,) + kept.shape[1:])
    )
    inner_edge = pick_rows(inner_ext, accepted_now, tail_inner.shape[1])
    shared_edge = pick_rows(shared_ext, accepted_now, tail_shared.shape[1])
    inner_bucket = jnp.einsum(
        "or,rqc->oqc", send_table, inner_edge, preferred_element_type=jnp.float32
    ).astype(jnp.bfloat16)
    shared_bucket = jnp.einsum(
        "or,rqc->oqc", send_table, shared_edge, preferred_element_type=jnp.float32
    ).astype(jnp.bfloat16)
    state_recv, inner_recv, shared_recv = (
        lax.all_to_all(state_bucket, "wide", split_axis=0, concat_axis=0, tiled=True),
        lax.all_to_all(inner_bucket, "wide", split_axis=0, concat_axis=0, tiled=True),
        lax.all_to_all(shared_bucket, "wide", split_axis=0, concat_axis=0, tiled=True),
    )
    senders = jnp.arange(slot_owner.shape[0], dtype=jnp.int32) // requests
    mine = slot_owner == wide_index
    picking = (
        (slot_rank[:, None] == jnp.arange(requests, dtype=jnp.int32)[None, :]) & mine[:, None]
    ).astype(jnp.bfloat16)
    from_sender = (senders[:, None] == jnp.arange(wide_count, dtype=jnp.int32)[None, :]).astype(
        jnp.bfloat16
    )
    selector = jnp.einsum(
        "jk,jw->kw", picking, from_sender, preferred_element_type=jnp.float32
    ).astype(jnp.bfloat16)
    kept_state = (
        jnp.dot(selector, state_recv.reshape(wide_count, -1), preferred_element_type=jnp.float32)
        .astype(jnp.bfloat16)
        .reshape(start_state.shape)
    )
    kept_tail_inner = jnp.einsum(
        "kw,wqc->kqc", selector, inner_recv, preferred_element_type=jnp.float32
    ).astype(jnp.bfloat16)
    kept_tail_shared = jnp.einsum(
        "kw,wqc->kqc", selector, shared_recv, preferred_element_type=jnp.float32
    ).astype(jnp.bfloat16)
    return (new_part, next_input, kept_state, kept_tail_inner, kept_tail_shared)


def solution(mesh):
    placed = (
        P("wide", "narrow"),
        P("wide", "narrow", None, None),
        P("wide", None, "narrow"),
        P("wide", None, None),
        P(),
        P(None, "narrow"),
        P(None, "narrow"),
        P(None, "narrow"),
        P("narrow"),
        P("narrow"),
        P(None, "narrow"),
        P("narrow"),
        P(),
        P(),
        P("narrow"),
        P("narrow"),
        P("narrow", None),
        P(),
        P(None, "narrow"),
        P(),
        P(),
        P(),
    )
    return jax.shard_map(
        local,
        mesh=mesh,
        in_specs=placed,
        out_specs=(
            P("wide", "narrow"),
            P("wide", "narrow"),
            P("wide", "narrow", None, None),
            P("wide", None, "narrow"),
            P("wide", None, None),
        ),
        check_vma=False,
    )
```

profile of v0, /device:TPU:24, one launch (start us, length us, event | category | flops | bytes accessed | tf_op | source)
XLA Modules:
  0.0 219.7 jit_solution(16669502044702229559)
XLA Ops:
  7.2 0.8 fusion.81
  8.8 1.3 gather_fusion
  10.1 0.8 and_select_fusion
  10.9 4.5 %gather_fusion.2 = s32[1024]{0:T(1024)S(1)} fusion(s32[1024]{0:T(1024)S(1)} %copy-done.1, s32[1024]{0:T(1024)S(1)} %fusion.81), kind=kCustom, calls=%fused_computation.1.clone | custom fusion | bytes 12288 | tf_op jit(solution)/shard_map/jit(_take)/gather | solution.py:162
  16.2 13.7 %all_gather.6 = bf16[256,1536]{0,1:T(8,128)(2,1)S(1)} all-gather(bf16[256,192]{0,1:T(8,128)(2,1)S(1)} %copy-done.7), channel_id=1, replica_groups=mesh['wide'=64,'narrow'=8] {'narrow'}, dimensions={1}, use_global_device_ids=true | all-gather | bytes 884736 | tf_op jit(solution)/shard_map/all_gather | solution.py:106
  30.5 1.9 convolution_convert_fusion.4
  34.4 16.6 %all-to-all-start.1 = ((bf16[64,3,192]{2,1,0:T(4,128)(2,1)}), bf16[64,3,192]{2,1,0:T(4,128)(2,1)}, u32[]{:S(2)}, u32[]{:S(2)}) async-start(bf16[64,3,192]{2,1,0:T(4,128)(2,1)} %copy.98), calls=%async_computation.1 | async-start | bytes 262144 | tf_op jit(solution)/shard_map/all_to_all | solution.py:183
  54.4 0.8 copy.95
  55.2 12.7 %all_gather.7 = bf16[256,256]{0,1:T(8,128)(2,1)S(1)} all-gather(bf16[256,32]{0,1:T(8,128)(2,1)S(1)} %convolution_convert_fusion.11), channel_id=1, replica_groups=mesh['wide'=64,'narrow'=8] {'narrow'}, dimensions={1}, use_global_device_ids=true | all-gather | bytes 147456 | tf_op jit(solution)/shard_map/all_gather | solution.py:121
  69.4 0.9 divide_multiply_fusion
  70.4 1.1 reshape.238
  71.5 2.2 %broadcast_multiply_fusion = f32[16,16,3,64]{3,2,1,0:T(4,128)} fusion(f32[16,16,3,64]{3,2,1,0:T(4,128)S(1)} %reshape.238, f32[16,16,3]{2,1,0:T(8,128)} %copy.95), kind=kLoop, calls=%fused_computation.72 | loop fusion | flops 49152 | bytes 396288 | tf_op jit(solution)/shard_map/rsh,rshp,rsn->rhpn/dot_general | solution.py:73
  73.7 1.5 divide_multiply_fusion.1
  75.2 12.7 %all-to-all-start.2 = ((bf16[64,3,256]{2,1,0:T(4,128)(2,1)}), bf16[64,3,256]{2,1,0:T(4,128)(2,1)S(1)}, u32[]{:S(2)}, u32[]{:S(2)}) async-start(bf16[64,3,256]{2,1,0:T(4,128)(2,1)} %copy.101), calls=%async_computation.2 | async-start | bytes 262144 | tf_op jit(solution)/shard_map/all_to_all | solution.py:184
  87.9 3.8 %add_convert_fusion = bf16[16,3,64,128]{3,2,1,0:T(8,128)(2,1)S(1)} fusion(bf16[16,3,64,128]{3,2,1,0:T(8,128)(2,1)S(1)} %copy-done.2, f32[16,3]{1,0:T(8,128)S(1)} %copy.93, f32[16,16,3,64]{3,2,1,0:T(4,128)} %broadcast_multiply_fusion, f32[16,16,256]{2,1,0:T(8,128)S(1)} %divide_multiply_fusion.1), kind=kOutput, calls=%fused_computation.21 | convolution fusion | flops 77070336 | bytes 1908736 | tf_op jit(solution)/shard_map/rsh,rshp,rsn->rhpn/dot_general | solution.py:73
  91.7 1.8 fusion.2
  93.5 2.5 %copy.114 = bf16[8,8,192,128]{3,2,1,0:T(8,128)(2,1)} copy(bf16[8,8,192,128]{3,1,2,0:T(8,128)(2,1)S(1)} %fusion.2) | data formatting | bytes 6291456
  96.0 2.8 %all-to-all-done.2 = bf16[64,3,256]{2,1,0:T(4,128)(2,1)S(1)} async-done(((bf16[64,3,256]{2,1,0:T(4,128)(2,1)}), bf16[64,3,256]{2,1,0:T(4,128)(2,1)S(1)}, u32[]{:S(2)}, u32[]{:S(2)}) %all-to-all-start.2) | async-done | bytes 98336 | tf_op jit(solution)/shard_map/all_to_all | solution.py:184
  98.8 10.3 %all-to-all-start = ((bf16[64,3,64,128]{3,2,1,0:T(8,128)(2,1)}), bf16[64,3,64,128]{3,2,1,0:T(8,128)(2,1)}, u32[]{:S(2)}, u32[]{:S(2)}) async-start(bf16[64,3,64,128]{3,2,1,0:T(8,128)(2,1)} %bitcast.87), calls=%async_computation | async-start | bytes 6291456 | tf_op jit(solution)/shard_map/all_to_all | solution.py:182
  109.7 0.8 copy.85
  111.1 1.7 convolution_multiply_fusion
  114.0 1.1 multiply_reduce_fusion
  115.1 14.5 %psum.14 = f32[256,1]{0,1:T(1,128)S(1)} all-reduce(f32[256,1]{0,1:T(1,128)S(1)} %bitcast.96), channel_id=1, replica_groups=mesh['wide'=64,'narrow'=8] {'narrow'}, use_global_device_ids=true, to_apply=%region_3.4 | all-reduce | flops 256 | bytes 2048 | tf_op jit(solution)/shard_map/psum | solution.py:144
  129.7 2.4 %convolution_convert_fusion.2 = bf16[256,1536]{1,0:T(8,128)(2,1)} fusion(bf16[192,1536]{1,0:T(8,128)(2,1)} %param.40, f32[192]{0:T(256)S(1)} %copy-done.24, f32[256]{0:T(256)S(1)} %bitcast.105, f32[256,192]{1,0:T(8,128)S(1)} %reshape.239, bf16[256,384]{1,0:T(8,128)(2,1)} %copy-done.6), kind=kOutput, calls=%fused_computation.7 | convolution fusion | flops 151830528 | bytes 1705728 | tf_op jit(solution)/shard_map/dot_general | solution.py:148
  132.2 18.0 %reduce-window.6 = s32[64,8,128]{2,1,0:T(8,128)S(1)} reduce-window(s32[64,8,128]{2,1,0:T(8,128)S(1)} %fusion.41, s32[]{:T(128)} %constant.71.clone.1), window={size=1x1x128 pad=0_0x0_0x127_0}, to_apply=%region_6.7 | reduce-window | flops 8323072 | bytes 524292 | tf_op jit(solution)/shard_map/reduce-window
  150.8 4.5 %gather_fusion.1 = s32[1024]{0:T(1024)S(1)} fusion(s32[1024]{0:T(1024)S(1)} %fusion.37, s32[1024]{0:T(1024)S(1)} %fusion.81), kind=kCustom, calls=%fused_computation.clone | custom fusion | bytes 12288 | tf_op jit(solution)/shard_map/jit(_take)/gather | solution.py:163
  156.2 1.7 convolution_convert_fusion.10
  158.6 45.9 %all-reduce.3.cloned.1.call-done = bf16[256,1536]{1,0:T(8,128)(2,1)} async-done(((bf16[256,1536]{1,0:T(8,128)(2,1)}), bf16[256,1536]{1,0:T(8,128)(2,1)}) %all-reduce.3.cloned.1.call-update) | async-done | bytes 786448 | tf_op jit(solution)/shard_map/psum | solution.py:149
  204.5 1.5 fusion.3
  206.8 1.3 convolution_convert_fusion.3
  208.2 3.7 %fusion.10 = bf16[2,8,192,128]{3,1,2,0:T(8,128)(2,1)S(1)} fusion(bf16[16,64]{1,0:T(8,128)(2,1)S(1)} %convolution_convert_fusion.12, bf16[8,8,192,128]{3,2,1,0:T(8,128)(2,1)} %bitcast.34), kind=kOutput, calls=%fused_computation.22 | convolution fusion | flops 50724864 | bytes 3934208 | tf_op jit(solution)/shard_map/dot_general | solution.py:198
  211.8 1.0 copy.116
  (117 shorter events, 14.1 us)
Async XLA Ops:
  7.2 199.7 %copy-start = (bf16[1536,403]{0,1:T(8,128)(2,1)S(1)}, bf16[1536,403]{0,1:T(8,128)(2,1)}, u32[]{:S(2)}) copy-start(bf16[1536,403]{0,1:T(8,128)(2,1)} %param.42) | copy-start | bytes 3714052
  7.2 3.7 %copy-start.1 = (s32[1024]{0:T(1024)S(1)}, s32[1024]{0:T(1024)}, u32[]{:S(2)}) copy-start(s32[1024]{0:T(1024)} %param.45) | copy-start | bytes 12292
  10.9 4.6 %copy-start.12 = (s32[1024]{0:T(1024)S(1)}, s32[1024]{0:T(1024)}, u32[]{:S(2)}) copy-start(s32[1024]{0:T(1024)} %param.43) | copy-start | bytes 12292
  10.9 5.3 %copy-start.10 = (bf16[16,3,192]{2,0,1:T(8,128)(2,1)S(1)}, bf16[16,3,192]{2,0,1:T(8,128)(2,1)}, u32[]{:S(2)}) copy-start(bf16[16,3,192]{2,0,1:T(8,128)(2,1)} %param.26) | copy-start | bytes 55300
  10.9 5.3 %copy-start.7 = (bf16[256,192]{0,1:T(8,128)(2,1)S(1)}, bf16[256,192]{0,1:T(8,128)(2,1)}, u32[]{:S(2)}) copy-start(bf16[256,192]{0,1:T(8,128)(2,1)} %param.24) | copy-start | bytes 294916
  16.1 52.2 %copy-start.15 = (s32[16]{0:T(128)}, s32[16]{0:T(128)S(1)}, u32[]{:S(2)}) copy-start(s32[16]{0:T(128)S(1)} %dynamic_slice.10) | copy-start | bytes 196
  16.2 14.3 %copy-start.22 = (f32[1536]{0:T(1024)S(1)}, f32[1536]{0:T(1024)}, u32[]{:S(2)}) copy-start(f32[1536]{0:T(1024)} %param.28) | copy-start | bytes 18436
  30.5 20.7 %copy-start.25 = (f32[3]{0:T(128)S(1)}, f32[3]{0:T(128)}, u32[]{:S(2)}) copy-start(f32[3]{0:T(128)} %param.33) | copy-start | bytes 40
  30.5 20.7 %copy-start.13 = (bf16[4,192]{1,0:T(4,128)(2,1)S(1)}, bf16[4,192]{1,0:T(4,128)(2,1)}, u32[]{:S(2)}) copy-start(bf16[4,192]{1,0:T(4,128)(2,1)} %param.34) | copy-start | bytes 4612
  30.5 20.7 %copy-start.14 = (bf16[4,256]{1,0:T(4,128)(2,1)S(1)}, bf16[4,256]{1,0:T(4,128)(2,1)}, u32[]{:S(2)}) copy-start(bf16[4,256]{1,0:T(4,128)(2,1)} %param.36) | copy-start | bytes 6148
  30.5 21.4 %copy-start.11 = (bf16[16,3,256]{2,0,1:T(8,128)(2,1)S(1)}, bf16[16,3,256]{2,0,1:T(8,128)(2,1)}, u32[]{:S(2)}) copy-start(bf16[16,3,256]{2,0,1:T(8,128)(2,1)} %param.27) | copy-start | bytes 73732
  30.5 21.4 %copy-start.21 = (bf16[1536,3]{0,1:T(4,128)(2,1)S(1)}, bf16[1536,3]{0,1:T(4,128)(2,1)}, u32[]{:S(2)}) copy-start(bf16[1536,3]{0,1:T(4,128)(2,1)} %param.31) | copy-start | bytes 27652
  32.5 0.7 copy-start.6
  32.5 19.8 %copy-start.20 = (bf16[1536,32]{0,1:T(8,128)(2,1)S(1)}, bf16[1536,32]{0,1:T(8,128)(2,1)}, u32[]{:S(2)}) copy-start(bf16[1536,32]{0,1:T(8,128)(2,1)} %param.30) | copy-start | bytes 294916
  34.4 40.8 %all-to-all-start.1 = ((bf16[64,3,192]{2,1,0:T(4,128)(2,1)}), bf16[64,3,192]{2,1,0:T(4,128)(2,1)}, u32[]{:S(2)}, u32[]{:S(2)}) async-start(bf16[64,3,192]{2,1,0:T(4,128)(2,1)} %copy.98), calls=%async_computation.1 | async-start | bytes 262144 | tf_op jit(solution)/shard_map/all_to_all | solution.py:183
  51.0 1.8 copy-start.19
  52.3 17.1 %copy-start.17 = (f32[192]{0:T(256)S(1)}, f32[192]{0:T(256)}, u32[]{:S(2)}) copy-start(f32[192]{0:T(256)} %param.35) | copy-start | bytes 2308
  68.0 0.7 copy-start.5
  69.4 18.5 %copy-start.2 = (bf16[16,3,64,128]{3,2,1,0:T(8,128)(2,1)S(1)}, bf16[16,3,64,128]{3,2,1,0:T(8,128)(2,1)}, u32[]{:S(2)}) copy-start(bf16[16,3,64,128]{3,2,1,0:T(8,128)(2,1)} %param.25) | copy-start | bytes 2359300
  71.5 2.2 %copy-start.3 = (f32[16,16,3,64]{3,2,1,0:T(4,128)}, f32[16,16,3,64]{3,2,1,0:T(4,128)S(1)}, u32[]{:S(2)}) copy-start(f32[16,16,3,64]{3,2,1,0:T(4,128)S(1)} %reshape.238) | copy-start | bytes 589828
  75.2 23.6 %all-to-all-start.2 = ((bf16[64,3,256]{2,1,0:T(4,128)(2,1)}), bf16[64,3,256]{2,1,0:T(4,128)(2,1)S(1)}, u32[]{:S(2)}, u32[]{:S(2)}) async-start(bf16[64,3,256]{2,1,0:T(4,128)(2,1)} %copy.101), calls=%async_computation.2 | async-start | bytes 262144 | tf_op jit(solution)/shard_map/all_to_all | solution.py:184
  98.8 109.4 %all-to-all-start = ((bf16[64,3,64,128]{3,2,1,0:T(8,128)(2,1)}), bf16[64,3,64,128]{3,2,1,0:T(8,128)(2,1)}, u32[]{:S(2)}, u32[]{:S(2)}) async-start(bf16[64,3,64,128]{3,2,1,0:T(8,128)(2,1)} %bitcast.87), calls=%async_computation | async-start | bytes 6291456 | tf_op jit(solution)/shard_map/all_to_all | solution.py:182
  109.0 3.8 %copy-start.26 = (f32[3]{0:T(128)S(1)}, f32[3]{0:T(128)}, u32[]{:S(2)}) copy-start(f32[3]{0:T(128)} %param.38) | copy-start | bytes 40
  109.1 95.4 %all-reduce.3.cloned.1.call-start = ((), (), s32[]{:S(2)}) async-start(), calls=%async_computation.3 | async-start | bytes 1572864 | tf_op jit(solution)/shard_map/psum | solution.py:149
  110.7 2.1 copy-start.4
  110.7 2.1 copy-start.8
  110.7 2.1 copy-start.9
  112.9 16.8 %copy-start.24 = (f32[192]{0:T(256)S(1)}, f32[192]{0:T(256)}, u32[]{:S(2)}) copy-start(f32[192]{0:T(256)} %param.39) | copy-start | bytes 2308
  150.8 4.6 %copy-start.16 = (pred[1024]{0:T(1024)(128)(4,1)S(1)}, pred[1024]{0:T(1024)(128)(4,1)}, u32[]{:S(2)}) copy-start(pred[1024]{0:T(1024)(128)(4,1)} %get-tuple-element.28) | copy-start | bytes 3076
  150.8 4.6 %copy-start.18 = (pred[1024]{0:T(1024)(128)(4,1)S(1)}, pred[1024]{0:T(1024)(128)(4,1)}, u32[]{:S(2)}) copy-start(pred[1024]{0:T(1024)(128)(4,1)} %get-tuple-element.26) | copy-start | bytes 3076
  156.2 50.7 %copy-start.23 = (f32[1536]{0:T(1024)S(1)}, f32[1536]{0:T(1024)}, u32[]{:S(2)}) copy-start(f32[1536]{0:T(1024)} %param.41) | copy-start | bytes 18436
Sparse Core Ops, SparseCore 0:
  132.2 72.1 all-reduce.2
where the time goes:
time: 220 us
  waiting for transfers between devices  48.7 us (22%)
  blocking collectives  41 us (19%)
  starting transfers between devices  39.6 us (18%)
  other arithmetic  30.4 us (14%)
  local copies, waits for them, and re-layouts  22.8 us (10%)
  matrix products  22.6 us (10%)
  between operations  14.6 us (7%)
    psum x1, waiting for transfers between devices, local(): lax.psum(partial_sum.astype(jnp.bfloat16), 'narrow').astype(jnp.float32)  45.9 us
    another operation x3, other arithmetic  18.2 us
    all_to_all x1, starting transfers between devices, local(): lax.all_to_all(inner_bucket, 'wide', split_axis=0, concat_axis=0, tiled=T...  16.6 us
    psum x1, blocking collectives, local(): squares = lax.psum(jnp.sum(gated * gated, axis=1, keepdims=True), 'narrow')  14.5 us
    all_gather x1, blocking collectives, local(): full_rows = lax.all_gather(hidden, 'narrow', axis=1, tiled=True)  13.7 us
    all_gather x1, blocking collectives, local(): shared_in = lax.all_gather(shared_piece, 'narrow', axis=1, tiled=True)  12.7 us
    all_to_all x1, starting transfers between devices, local(): lax.all_to_all(shared_bucket, 'wide', split_axis=0, concat_axis=0, tiled=...  12.7 us
    all_to_all x1, starting transfers between devices, local(): lax.all_to_all(state_bucket, 'wide', split_axis=0, concat_axis=0, tiled=T...  10.3 us
  transfers between devices with their start and end apart: 4, of which 2 were waited for; matrix products, arithmetic and copies ran while one was open for 26% of the time, Pallas kernels for 0%

commit v1 on v0

--- a/solution.py
+++ b/solution.py
@@ -5,6 +5,24 @@
 
 EPSILON = 1e-05
 HIGHEST = lax.Precision.HIGHEST
+
+
+def gather_around(value, axis, dim):
+    ways, here, turn = (lax.axis_size(axis), lax.axis_index(axis), value.shape[dim])
+    shape = [n * ways if d == dim else n for d, n in enumerate(value.shape)]
+    full = lax.dynamic_update_slice_in_dim(
+        jnp.zeros(shape, value.dtype), value, here * turn, axis=dim
+    )
+    going_up = going_down = value
+    for far in range(1, ways // 2 + 1):
+        going_up = lax.ppermute(going_up, axis, [(d, (d + 1) % ways) for d in range(ways)])
+        full = lax.dynamic_update_slice_in_dim(full, going_up, (here - far) % ways * turn, axis=dim)
+        if 2 * far < ways:
+            going_down = lax.ppermute(going_down, axis, [(d, (d - 1) % ways) for d in range(ways)])
+            full = lax.dynamic_update_slice_in_dim(
+                full, going_down, (here + far) % ways * turn, axis=dim
+            )
+    return full
 
 
 def root_norm(values, gain):
@@ -103,7 +121,7 @@
     wide_index = lax.axis_index("wide")
     wide_count = lax.axis_size("wide")
     narrow_count = lax.axis_size("narrow")
-    full_rows = lax.all_gather(hidden, "narrow", axis=1, tiled=True)
+    full_rows = gather_around(hidden, "narrow", 1)
     normed_in = root_norm(full_rows, input_gain)
     tokens = full_rows.shape[0]
     requests = start_state.shape[0]

time: 220 us -> 266 us (1.21)
  the two profiles are of different devices: /device:TPU:24 before, /device:TPU:8 now
where the time goes in v1:
time: 266 us; the launch traced here: 264 us
  waiting for transfers between devices  83 us (31%)
  other arithmetic  42.9 us (16%)
  starting transfers between devices  40.7 us (15%)
  local copies, waits for them, and re-layouts  34.1 us (13%)
  blocking collectives  26.2 us (10%)
  matrix products  22.5 us (8%)
  between operations  14.9 us (6%)
    psum x1, waiting for transfers between devices, local(): lax.psum(partial_sum.astype(jnp.bfloat16), 'narrow').astype(jnp.float32)  68.5 us
    another operation x3, other arithmetic  31 us
    all_to_all x1, starting transfers between devices, local(): lax.all_to_all(inner_bucket, 'wide', split_axis=0, concat_axis=0, tiled=T...  16.8 us
    psum x1, blocking collectives, local(): squares = lax.psum(jnp.sum(gated * gated, axis=1, keepdims=True), 'narrow')  13.4 us
    all_gather x1, blocking collectives, local(): shared_in = lax.all_gather(shared_piece, 'narrow', axis=1, tiled=True)  12.7 us
    all_to_all x1, starting transfers between devices, local(): lax.all_to_all(state_bucket, 'wide', split_axis=0, concat_axis=0, tiled=T...  9.23 us
    ppermute x3, starting transfers between devices, gather_around(): lax.ppermute(going_down, axis, [(d, (d - 1) % ways) for d in range(ways)])  8.24 us
    all_to_all x1, starting transfers between devices, local(): lax.all_to_all(shared_bucket, 'wide', split_axis=0, concat_axis=0, tiled=...  6.37 us
  transfers between devices with their start and end apart: 11, of which 6 were waited for; matrix products, arithmetic and copies ran while one was open for 32% of the time, Pallas kernels for 0%

profile of v1, /device:TPU:8, one launch (start us, length us, event | category | flops | bytes accessed | tf_op | source)
XLA Modules:
  0.0 264.2 jit_solution(6247746344815310584)
XLA Ops:
  8.3 2.2 collective-permute-start.1
  12.0 1.3 gather_fusion
  14.3 4.5 %gather_fusion.2 = s32[1024]{0:T(1024)S(1)} fusion(s32[1024]{0:T(1024)S(1)} %copy-done.1, s32[1024]{0:T(1024)S(1)} %fusion.81), kind=kCustom, calls=%fused_computation.1.clone | custom fusion | bytes 12288 | tf_op jit(solution)/shard_map/jit(_take)/gather | solution.py:180
  20.0 3.0 %collective-permute-start.3 = (bf16[256,192]{1,0:T(8,128)(2,1)S(1)}, bf16[256,192]{1,0:T(8,128)(2,1)S(1)}, u32[]{:S(2)}, u32[]{:S(2)}) collective-permute-start(bf16[256,192]{1,0:T(8,128)(2,1)S(1)} %collective-permute-done.1), channel_id=1, source_target_pairs={{0,7},{1,0},{2,1},{3,2},{4,3},{5,4},{6,5},{7,6},{8,15},{9,8},{10,9... | collective-permute-start | bytes 294920 | tf_op jit(solution)/shard_map/ppermute | solution.py:21
  23.0 2.0 collective-permute-done.2
  25.5 3.1 %collective-permute-start.5 = (bf16[256,192]{1,0:T(8,128)(2,1)S(1)}, bf16[256,192]{1,0:T(8,128)(2,1)S(1)}, u32[]{:S(2)}, u32[]{:S(2)}) collective-permute-start(bf16[256,192]{1,0:T(8,128)(2,1)S(1)} %collective-permute-done.3), channel_id=1, source_target_pairs={{0,7},{1,0},{2,1},{3,2},{4,3},{5,4},{6,5},{7,6},{8,15},{9,8},{10,9... | collective-permute-start | bytes 294920 | tf_op jit(solution)/shard_map/ppermute | solution.py:21
  28.6 2.0 collective-permute-done.4
  33.4 1.5 dynamic_update_slice.26
  36.9 1.5 dynamic_update_slice.29
  38.5 1.5 dynamic_update_slice.30
  44.7 12.7 %all_gather.3 = bf16[256,256]{0,1:T(8,128)(2,1)S(1)} all-gather(bf16[256,32]{0,1:T(8,128)(2,1)S(1)} %convolution_convert_fusion.11), channel_id=1, replica_groups=mesh['wide'=64,'narrow'=8] {'narrow'}, dimensions={1}, use_global_device_ids=true | all-gather | bytes 147456 | tf_op jit(solution)/shard_map/all_gather | solution.py:139
  58.8 1.9 convolution_convert_fusion.4
  62.1 16.8 %all-to-all-start.1 = ((bf16[64,3,192]{2,1,0:T(4,128)(2,1)}), bf16[64,3,192]{2,1,0:T(4,128)(2,1)}, u32[]{:S(2)}, u32[]{:S(2)}) async-start(bf16[64,3,192]{2,1,0:T(4,128)(2,1)} %copy.106), calls=%async_computation.1 | async-start | bytes 262144 | tf_op jit(solution)/shard_map/all_to_all | solution.py:201
  81.0 2.2 broadcast_multiply_fusion
  83.2 1.5 divide_multiply_fusion.1
  84.7 6.4 %all-to-all-done.1 = bf16[64,3,192]{2,1,0:T(4,128)(2,1)} async-done(((bf16[64,3,192]{2,1,0:T(4,128)(2,1)}), bf16[64,3,192]{2,1,0:T(4,128)(2,1)}, u32[]{:S(2)}, u32[]{:S(2)}) %all-to-all-start.1) | async-done | bytes 73760 | tf_op jit(solution)/shard_map/all_to_all | solution.py:201
  91.1 6.4 %all-to-all-start.2 = ((bf16[64,3,256]{2,1,0:T(4,128)(2,1)}), bf16[64,3,256]{2,1,0:T(4,128)(2,1)S(1)}, u32[]{:S(2)}, u32[]{:S(2)}) async-start(bf16[64,3,256]{2,1,0:T(4,128)(2,1)} %copy.109), calls=%async_computation.2 | async-start | bytes 262144 | tf_op jit(solution)/shard_map/all_to_all | solution.py:202
  97.5 3.8 %add_convert_fusion = bf16[16,3,64,128]{3,2,1,0:T(8,128)(2,1)S(1)} fusion(bf16[16,3,64,128]{3,2,1,0:T(8,128)(2,1)S(1)} %copy-done.2, f32[16,3]{1,0:T(8,128)S(1)} %copy.101, f32[16,16,3,64]{3,2,1,0:T(4,128)} %broadcast_multiply_fusion, f32[16,16,256]{2,1,0:T(8,128)S(1)} %divide_multiply_fusion.1), kind=kOutput, calls=%fused_computation.21 | convolution fusion | flops 77070336 | bytes 1908736 | tf_op jit(solution)/shard_map/rsh,rshp,rsn->rhpn/dot_general | solution.py:91
  101.3 1.7 fusion.2
  103.0 2.5 copy.122
  105.5 3.6 %all-to-all-done.2 = bf16[64,3,256]{2,1,0:T(4,128)(2,1)S(1)} async-done(((bf16[64,3,256]{2,1,0:T(4,128)(2,1)}), bf16[64,3,256]{2,1,0:T(4,128)(2,1)S(1)}, u32[]{:S(2)}, u32[]{:S(2)}) %all-to-all-start.2) | async-done | bytes 98336 | tf_op jit(solution)/shard_map/all_to_all | solution.py:202
  109.8 9.2 %all-to-all-start = ((bf16[64,3,64,128]{3,2,1,0:T(8,128)(2,1)}), bf16[64,3,64,128]{3,2,1,0:T(8,128)(2,1)}, u32[]{:S(2)}, u32[]{:S(2)}) async-start(bf16[64,3,64,128]{3,2,1,0:T(8,128)(2,1)} %bitcast.87), calls=%async_computation | async-start | bytes 6291456 | tf_op jit(solution)/shard_map/all_to_all | solution.py:200
  119.8 30.8 %reduce-window.6 = s32[64,8,128]{2,1,0:T(8,128)S(1)} reduce-window(s32[64,8,128]{2,1,0:T(8,128)} %fusion.41, s32[]{:T(128)} %constant.111.clone.1), window={size=1x1x128 pad=0_0x0_0x127_0}, to_apply=%region_6.7 | reduce-window | flops 8323072 | bytes 524292 | tf_op jit(solution)/shard_map/reduce-window
  152.9 4.5 %gather_fusion.1 = s32[1024]{0:T(1024)S(1)} fusion(s32[1024]{0:T(1024)S(1)} %fusion.37, s32[1024]{0:T(1024)S(1)} %fusion.81), kind=kCustom, calls=%fused_computation.clone | custom fusion | bytes 12288 | tf_op jit(solution)/shard_map/jit(_take)/gather | solution.py:181
  159.0 1.7 convolution_multiply_fusion
  162.1 13.4 %psum.14 = f32[256,1]{0,1:T(1,128)S(1)} all-reduce(f32[256,1]{0,1:T(1,128)S(1)} %bitcast.96), channel_id=1, replica_groups=mesh['wide'=64,'narrow'=8] {'narrow'}, use_global_device_ids=true, to_apply=%region_3.4 | all-reduce | flops 256 | bytes 2048 | tf_op jit(solution)/shard_map/psum | solution.py:162
  175.6 2.4 convolution_convert_fusion.2
  178.1 1.7 convolution_convert_fusion.10
  180.5 68.5 %all-reduce.3.cloned.1.call-done = bf16[256,1536]{1,0:T(8,128)(2,1)} async-done(((bf16[256,1536]{1,0:T(8,128)(2,1)}), bf16[256,1536]{1,0:T(8,128)(2,1)}) %all-reduce.3.cloned.1.call-update) | async-done | bytes 786448 | tf_op jit(solution)/shard_map/psum | solution.py:167
  248.9 1.5 fusion.3
  251.3 1.3 convolution_convert_fusion.3
  252.6 3.7 %fusion.10 = bf16[2,8,192,128]{3,1,2,0:T(8,128)(2,1)S(1)} fusion(bf16[16,64]{1,0:T(8,128)(2,1)S(1)} %convolution_convert_fusion.12, bf16[8,8,192,128]{3,2,1,0:T(8,128)(2,1)} %bitcast.34), kind=kOutput, calls=%fused_computation.22 | convolution fusion | flops 50724864 | bytes 3934208 | tf_op jit(solution)/shard_map/dot_general | solution.py:216
  (139 shorter events, 28.3 us)
Async XLA Ops:
  7.2 244.1 %copy-start = (bf16[1536,403]{0,1:T(8,128)(2,1)S(1)}, bf16[1536,403]{0,1:T(8,128)(2,1)}, u32[]{:S(2)}) copy-start(bf16[1536,403]{0,1:T(8,128)(2,1)} %param.42) | copy-start | bytes 3714052
  7.2 7.0 %copy-start.1 = (s32[1024]{0:T(1024)S(1)}, s32[1024]{0:T(1024)}, u32[]{:S(2)}) copy-start(s32[1024]{0:T(1024)} %param.45) | copy-start | bytes 12292
  8.3 11.7 %collective-permute-start.1 = (bf16[256,192]{1,0:T(8,128)(2,1)S(1)}, bf16[256,192]{1,0:T(8,128)(2,1)S(1)}, u32[]{:S(2)}, u32[]{:S(2)}) collective-permute-start(bf16[256,192]{1,0:T(8,128)(2,1)S(1)} %copy.85), channel_id=1, source_target_pairs={{0,7},{1,0},{2,1},{3,2},{4,3},{5,4},{6,5},{7,6},{8,15},{9,8},{10,9... | collective-permute-start | bytes 294920 | tf_op jit(solution)/shard_map/ppermute | solution.py:21
  10.5 8.9 %collective-permute-start = (bf16[256,192]{1,0:T(8,128)(2,1)S(1)}, bf16[256,192]{1,0:T(8,128)(2,1)S(1)}, u32[]{:S(2)}, u32[]{:S(2)}) collective-permute-start(bf16[256,192]{1,0:T(8,128)(2,1)S(1)} %copy.85), channel_id=1, source_target_pairs={{0,1},{1,2},{2,3},{3,4},{4,5},{5,6},{6,7},{7,0},{8,9},{9,10},{10,1... | collective-permute-start | bytes 294920 | tf_op jit(solution)/shard_map/ppermute | solution.py:18
  14.2 4.6 %copy-start.12 = (s32[1024]{0:T(1024)S(1)}, s32[1024]{0:T(1024)}, u32[]{:S(2)}) copy-start(s32[1024]{0:T(1024)} %param.43) | copy-start | bytes 12292
  14.2 5.2 %copy-start.13 = (bf16[4,192]{1,0:T(4,128)(2,1)S(1)}, bf16[4,192]{1,0:T(4,128)(2,1)}, u32[]{:S(2)}) copy-start(bf16[4,192]{1,0:T(4,128)(2,1)} %param.34) | copy-start | bytes 4612
  14.2 5.2 %copy-start.14 = (bf16[4,256]{1,0:T(4,128)(2,1)S(1)}, bf16[4,256]{1,0:T(4,128)(2,1)}, u32[]{:S(2)}) copy-start(bf16[4,256]{1,0:T(4,128)(2,1)} %param.36) | copy-start | bytes 6148
  14.3 16.4 %copy-start.25 = (f32[3]{0:T(128)S(1)}, f32[3]{0:T(128)}, u32[]{:S(2)}) copy-start(f32[3]{0:T(128)} %param.33) | copy-start | bytes 40
  14.3 16.7 %copy-start.10 = (bf16[16,3,192]{2,0,1:T(8,128)(2,1)S(1)}, bf16[16,3,192]{2,0,1:T(8,128)(2,1)}, u32[]{:S(2)}) copy-start(bf16[16,3,192]{2,0,1:T(8,128)(2,1)} %param.26) | copy-start | bytes 55300
  14.3 16.7 %copy-start.11 = (bf16[16,3,256]{2,0,1:T(8,128)(2,1)S(1)}, bf16[16,3,256]{2,0,1:T(8,128)(2,1)}, u32[]{:S(2)}) copy-start(bf16[16,3,256]{2,0,1:T(8,128)(2,1)} %param.27) | copy-start | bytes 73732
  19.4 5.6 %collective-permute-start.2 = (bf16[256,192]{1,0:T(8,128)(2,1)S(1)}, bf16[256,192]{1,0:T(8,128)(2,1)S(1)}, u32[]{:S(2)}, u32[]{:S(2)}) collective-permute-start(bf16[256,192]{1,0:T(8,128)(2,1)S(1)} %collective-permute-done), channel_id=1, source_target_pairs={{0,1},{1,2},{2,3},{3,4},{4,5},{5,6},{6,7},{7,0},{8,9},{9,10},{10,1... | collective-permute-start | bytes 294920 | tf_op jit(solution)/shard_map/ppermute | solution.py:18
  20.0 5.5 %collective-permute-start.3 = (bf16[256,192]{1,0:T(8,128)(2,1)S(1)}, bf16[256,192]{1,0:T(8,128)(2,1)S(1)}, u32[]{:S(2)}, u32[]{:S(2)}) collective-permute-start(bf16[256,192]{1,0:T(8,128)(2,1)S(1)} %collective-permute-done.1), channel_id=1, source_target_pairs={{0,7},{1,0},{2,1},{3,2},{4,3},{5,4},{6,5},{7,6},{8,15},{9,8},{10,9... | collective-permute-start | bytes 294920 | tf_op jit(solution)/shard_map/ppermute | solution.py:21
  25.0 5.6 %collective-permute-start.4 = (bf16[256,192]{1,0:T(8,128)(2,1)S(1)}, bf16[256,192]{1,0:T(8,128)(2,1)S(1)}, u32[]{:S(2)}, u32[]{:S(2)}) collective-permute-start(bf16[256,192]{1,0:T(8,128)(2,1)S(1)} %collective-permute-done.2), channel_id=1, source_target_pairs={{0,1},{1,2},{2,3},{3,4},{4,5},{5,6},{6,7},{7,0},{8,9},{9,10},{10,1... | collective-permute-start | bytes 294920 | tf_op jit(solution)/shard_map/ppermute | solution.py:18
  25.5 12.9 %collective-permute-start.5 = (bf16[256,192]{1,0:T(8,128)(2,1)S(1)}, bf16[256,192]{1,0:T(8,128)(2,1)S(1)}, u32[]{:S(2)}, u32[]{:S(2)}) collective-permute-start(bf16[256,192]{1,0:T(8,128)(2,1)S(1)} %collective-permute-done.3), channel_id=1, source_target_pairs={{0,7},{1,0},{2,1},{3,2},{4,3},{5,4},{6,5},{7,6},{8,15},{9,8},{10,9... | collective-permute-start | bytes 294920 | tf_op jit(solution)/shard_map/ppermute | solution.py:21
  30.6 9.4 %collective-permute-start.6 = (bf16[256,192]{1,0:T(8,128)(2,1)S(1)}, bf16[256,192]{1,0:T(8,128)(2,1)S(1)}, u32[]{:S(2)}, u32[]{:S(2)}) collective-permute-start(bf16[256,192]{1,0:T(8,128)(2,1)S(1)} %collective-permute-done.4), channel_id=1, source_target_pairs={{0,1},{1,2},{2,3},{3,4},{4,5},{5,6},{6,7},{7,0},{8,9},{9,10},{10,1... | collective-permute-start | bytes 294920 | tf_op jit(solution)/shard_map/ppermute | solution.py:18
  30.9 30.2 %copy-start.15 = (s32[16]{0:T(128)}, s32[16]{0:T(128)S(1)}, u32[]{:S(2)}) copy-start(s32[16]{0:T(128)S(1)} %dynamic_slice.10) | copy-start | bytes 196
  31.1 10.3 %copy-start.21 = (bf16[1536,3]{0,1:T(4,128)(2,1)S(1)}, bf16[1536,3]{0,1:T(4,128)(2,1)}, u32[]{:S(2)}) copy-start(bf16[1536,3]{0,1:T(4,128)(2,1)} %param.31) | copy-start | bytes 27652
  31.1 10.3 %copy-start.22 = (f32[1536]{0:T(1024)S(1)}, f32[1536]{0:T(1024)}, u32[]{:S(2)}) copy-start(f32[1536]{0:T(1024)} %param.28) | copy-start | bytes 18436
  36.9 4.9 %copy-start.20 = (bf16[1536,32]{0,1:T(8,128)(2,1)S(1)}, bf16[1536,32]{0,1:T(8,128)(2,1)}, u32[]{:S(2)}) copy-start(bf16[1536,32]{0,1:T(8,128)(2,1)} %param.30) | copy-start | bytes 294916
  57.5 3.2 %copy-start.5 = (bf16[256,256]{1,0:T(8,128)(2,1)}, bf16[256,256]{1,0:T(8,128)(2,1)S(1)}, u32[]{:S(2)}) copy-start(bf16[256,256]{1,0:T(8,128)(2,1)S(1)} %copy.88) | copy-start | bytes 393220
  58.8 20.1 %copy-start.17 = (f32[192]{0:T(256)S(1)}, f32[192]{0:T(256)}, u32[]{:S(2)}) copy-start(f32[192]{0:T(256)} %param.35) | copy-start | bytes 2308
  62.1 28.9 %all-to-all-start.1 = ((bf16[64,3,192]{2,1,0:T(4,128)(2,1)}), bf16[64,3,192]{2,1,0:T(4,128)(2,1)}, u32[]{:S(2)}, u32[]{:S(2)}) async-start(bf16[64,3,192]{2,1,0:T(4,128)(2,1)} %copy.106), calls=%async_computation.1 | async-start | bytes 262144 | tf_op jit(solution)/shard_map/all_to_all | solution.py:201
  78.9 18.5 %copy-start.2 = (bf16[16,3,64,128]{3,2,1,0:T(8,128)(2,1)S(1)}, bf16[16,3,64,128]{3,2,1,0:T(8,128)(2,1)}, u32[]{:S(2)}) copy-start(bf16[16,3,64,128]{3,2,1,0:T(8,128)(2,1)} %param.25) | copy-start | bytes 2359300
  91.1 18.1 %all-to-all-start.2 = ((bf16[64,3,256]{2,1,0:T(4,128)(2,1)}), bf16[64,3,256]{2,1,0:T(4,128)(2,1)S(1)}, u32[]{:S(2)}, u32[]{:S(2)}) async-start(bf16[64,3,256]{2,1,0:T(4,128)(2,1)} %copy.109), calls=%async_computation.2 | async-start | bytes 262144 | tf_op jit(solution)/shard_map/all_to_all | solution.py:202
  109.8 142.8 %all-to-all-start = ((bf16[64,3,64,128]{3,2,1,0:T(8,128)(2,1)}), bf16[64,3,64,128]{3,2,1,0:T(8,128)(2,1)}, u32[]{:S(2)}, u32[]{:S(2)}) async-start(bf16[64,3,64,128]{3,2,1,0:T(8,128)(2,1)} %bitcast.87), calls=%async_computation | async-start | bytes 6291456 | tf_op jit(solution)/shard_map/all_to_all | solution.py:200
  119.0 129.9 %all-reduce.3.cloned.1.call-start = ((), (), s32[]{:S(2)}) async-start(), calls=%async_computation.3 | async-start | bytes 1572864 | tf_op jit(solution)/shard_map/psum | solution.py:167
  152.9 4.6 %copy-start.16 = (pred[1024]{0:T(1024)(128)(4,1)S(1)}, pred[1024]{0:T(1024)(128)(4,1)}, u32[]{:S(2)}) copy-start(pred[1024]{0:T(1024)(128)(4,1)} %get-tuple-element.28) | copy-start | bytes 3076
  152.9 4.6 %copy-start.18 = (pred[1024]{0:T(1024)(128)(4,1)S(1)}, pred[1024]{0:T(1024)(128)(4,1)}, u32[]{:S(2)}) copy-start(pred[1024]{0:T(1024)(128)(4,1)} %get-tuple-element.26) | copy-start | bytes 3076
  157.4 3.3 %copy-start.26 = (f32[3]{0:T(128)S(1)}, f32[3]{0:T(128)}, u32[]{:S(2)}) copy-start(f32[3]{0:T(128)} %param.38) | copy-start | bytes 40
  160.8 14.8 %copy-start.24 = (f32[192]{0:T(256)S(1)}, f32[192]{0:T(256)}, u32[]{:S(2)}) copy-start(f32[192]{0:T(256)} %param.39) | copy-start | bytes 2308
  175.6 4.1 %copy-start.7 = (bf16[64,3,256]{2,1,0:T(4,128)(2,1)S(1)}, bf16[64,3,256]{2,1,0:T(4,128)(2,1)}, u32[]{:S(2)}) copy-start(bf16[64,3,256]{2,1,0:T(4,128)(2,1)} %copy-done.6) | copy-start | bytes 294916
  178.0 73.2 %copy-start.23 = (f32[1536]{0:T(1024)S(1)}, f32[1536]{0:T(1024)}, u32[]{:S(2)}) copy-start(f32[1536]{0:T(1024)} %param.41) | copy-start | bytes 18436
  (6 other events, 8.4 us)
Sparse Core Ops, SparseCore 0:
  178.2 70.7 all-reduce.2
